TPU v7x, 256 devices: a whole 4x4x8 slice. The times are simulated.
256 devices in a mesh: bag: 64 (over y, z, core), seq: 4 (over x).
Axes of the slice: x: 4, y: 4, z: 8, core: 2. Of those that a mesh axis runs over, the one named last changes fastest.
Arguments:
- video: bfloat16 [32768, 5120], P('bag'), may hold values from -6 to 6
- w_query: bfloat16 [5120, 5120], P('bag', 'seq'), may hold values from -0.078125 to 0.078125
- cond_kv: bfloat16 [64, 512, 2, 5120], P('bag', None, None, 'seq'), may hold values from -400 to 400, as said below
- neg_kv: bfloat16 [512, 2, 5120], P('bag', None, 'seq'), may hold values from -400 to 400, as said below
- prompt_len: int32 [64], P('bag'), may hold values from 1 to 512
- neg_len: int32 [1], replicated, may hold values from 1 to 512
Outputs:
- guided: bfloat16 [32768, 5120], P('bag', 'seq')
Inputs may be any that keep to these rules, and one draw needn't show every extreme that they name: `cond_kv`: finite keys and values. `neg_kv`: finite keys and values.
All inputs are finite; a program needn't handle non-finite values.
Results may differ from a plain program's by a relative error of at most 0.012.
The roundings to bfloat16 on the way count: a program that leaves them out, or rounds other values in their place, can miss the bound.
Values may be sent and summed in bfloat16 or wider, within the bound.
No kernel may reach another device: no remote copies, remote signals or barrier semaphores. Data moves between devices by JAX's collectives and lax.ppermute only.
A program may use at most 128 MiB of HBM per device.

v0:
```python
import jax
import jax.numpy as jnp
from jax import lax
from jax.sharding import PartitionSpec as P

DM = 5120
HD = 128
guidance_scale = 5.0


def layer_norm(video):
    values = video.astype(jnp.float32)
    center = values - jnp.mean(values, axis=-1, keepdims=True)
    spread = jnp.mean(center * center, axis=-1, keepdims=True)
    return (center * lax.rsqrt(spread + 1e-06)).astype(jnp.bfloat16)


def negative_rows(neg_kv):
    return lax.all_gather(neg_kv, "bag", axis=0, tiled=True)


def attend(query_rms, keys, values, length):
    tok_rows = query_rms.shape[0]
    key_rows = keys.shape[0]
    local_heads = query_rms.shape[1] // HD
    q_heads = query_rms.reshape(tok_rows, local_heads, HD)
    k_heads = keys.reshape(key_rows, local_heads, HD)
    v_heads = values.reshape(key_rows, local_heads, HD)
    scores = jnp.einsum(
        "thd,shd->hts", q_heads, k_heads, preferred_element_type=jnp.float32
    ) / jnp.sqrt(jnp.float32(HD))
    live = (jnp.arange(key_rows, dtype=jnp.int32) < length)[None, None, :]
    scores = jnp.where(live, scores, jnp.float32(-1e30))
    top = jnp.max(scores, axis=-1, keepdims=True)
    weights = jnp.where(live, jnp.exp(scores - top), jnp.float32(0.0))
    weights = (weights / jnp.sum(weights, axis=-1, keepdims=True)).astype(jnp.bfloat16)
    mixed = jnp.einsum("hts,shd->thd", weights, v_heads, preferred_element_type=jnp.float32)
    return mixed.reshape(tok_rows, local_heads * HD)


def body(video, w_query, cond_kv, neg_kv, prompt_len, neg_len):
    normed = layer_norm(video)
    gathered = lax.all_gather(w_query, "bag", axis=0, tiled=True)
    query = jnp.dot(normed, gathered, preferred_element_type=jnp.float32)
    squares = lax.psum(jnp.sum(query * query, axis=1), "seq")
    query_rms = (query * lax.rsqrt(squares / DM + 1e-06)[:, None]).astype(jnp.bfloat16)
    negative = negative_rows(neg_kv)
    cond = attend(query_rms, cond_kv[0, :, 0], cond_kv[0, :, 1], prompt_len[0])
    uncond = attend(query_rms, negative[:, 0], negative[:, 1], neg_len[0])
    return (uncond + guidance_scale * (cond - uncond)).astype(jnp.bfloat16)


def solution(mesh):
    in_specs = (
        P("bag", None),
        P("bag", "seq"),
        P("bag", None, None, "seq"),
        P("bag", None, "seq"),
        P("bag"),
        P(),
    )
    out_specs = P("bag", "seq")
    return jax.shard_map(body, mesh=mesh, in_specs=in_specs, out_specs=out_specs, check_vma=False)
```

profile of v0, /device:TPU:32, one launch (start us, length us, event | category | flops | bytes accessed | tf_op | source)
XLA Modules:
  0.0 257.8 jit_solution(1056586922885122837)
XLA Ops:
  6.5 0.0 all-gather.5.cloned.1.call-start
  6.5 0.7 all-gather.5.cloned.1.call-update
  7.3 0.0 all-gather.3.cloned.1.call-start
  7.3 0.7 all-gather.3.cloned.1.call-update
  9.3 7.7 %fusion.28 = (bf16[1,512,1,1280]{3,2,1,0:T(2,128)(2,1)}, bf16[1,512,1,1280]{3,2,1,0:T(2,128)(2,1)S(1)}) fusion(bf16[1,512,2,1280]{3,2,1,0:T(2,128)(2,1)} %param.8), kind=kLoop, calls=%fused_computation.41 | loop fusion | bytes 5242880 | tf_op jit(solution)/shard_map/slice | solution.py:48
  17.0 6.2 %copy.50 = bf16[1,512,1,1280]{1,3,2,0:T(8,128)(2,1)} copy(bf16[1,512,1,1280]{3,2,1,0:T(2,128)(2,1)} %get-tuple-element.5) | data formatting | bytes 2621440
  23.1 3.8 %copy.38 = bf16[1,512,1,1280]{1,3,2,0:T(8,128)(2,1)} copy(bf16[1,512,1,1280]{3,2,1,0:T(2,128)(2,1)S(1)} %get-tuple-element.6) | data formatting | bytes 2621440 | tf_op jit(solution)/shard_map/slice | solution.py:48
  27.0 3.3 %convert_reduce_fusion = f32[512]{0:T(512)S(1)} fusion(bf16[512,5120]{1,0:T(8,128)(2,1)} %param.6), kind=kLoop, calls=%fused_computation.3 | loop fusion | flops 5242368 | bytes 5244928 | tf_op jit(solution)/shard_map/reduce_sum | solution.py:13
  30.2 4.0 %fusion.4 = f32[512]{0:T(512)S(1)} fusion(bf16[512,5120]{1,0:T(8,128)(2,1)} %param.6, f32[512]{0:T(512)S(1)} %broadcast_multiply_fusion), kind=kLoop, calls=%fused_computation.6 | loop fusion | flops 10485248 | bytes 5246976 | tf_op jit(solution)/shard_map/reduce_sum | solution.py:14
  34.2 55.3 %all-gather.5.cloned.1.call-done = bf16[512,2,1280]{2,1,0:T(2,128)(2,1)} async-done(((bf16[8,2,1280]{2,1,0:T(2,128)(2,1)}), bf16[512,2,1280]{2,1,0:T(2,128)(2,1)}) %all-gather.5.cloned.1.call-update) | async-done | bytes 2621456 | tf_op jit(solution)/shard_map/all_gather | solution.py:19
  89.5 7.7 %fusion.29 = (bf16[512,1,1280]{2,1,0:T(2,128)(2,1)}, bf16[512,1,1280]{2,1,0:T(2,128)(2,1)S(1)}) fusion(bf16[512,2,1280]{2,1,0:T(2,128)(2,1)} %all-gather.5.cloned.1.call-done), kind=kLoop, calls=%fused_computation.42 | loop fusion | bytes 5242880 | tf_op jit(solution)/shard_map/slice | solution.py:49
  97.2 6.2 %copy.49 = bf16[512,1,1280]{0,2,1:T(8,128)(2,1)} copy(bf16[512,1,1280]{2,1,0:T(2,128)(2,1)} %get-tuple-element.7) | data formatting | bytes 2621440
  103.4 3.7 %copy.33 = bf16[512,1,1280]{0,2,1:T(8,128)(2,1)} copy(bf16[512,1,1280]{2,1,0:T(2,128)(2,1)S(1)} %get-tuple-element.8) | data formatting | bytes 2621440 | tf_op jit(solution)/shard_map/slice | solution.py:49
  107.1 74.0 %all-gather.3.cloned.1.call-done = bf16[5120,1280]{1,0:T(8,128)(2,1)} async-done(((bf16[80,1280]{1,0:T(8,128)(2,1)}), bf16[5120,1280]{1,0:T(8,128)(2,1)}) %all-gather.3.cloned.1.call-update) | async-done | bytes 13107216 | tf_op jit(solution)/shard_map/all_gather | solution.py:43
  181.2 14.0 %multiply_reduce_fusion = (f32[512]{0:T(512)S(1)}, f32[512,1280]{1,0:T(8,128)}) fusion(bf16[5120,1280]{1,0:T(8,128)(2,1)} %all-gather.3.cloned.1.call-done, bf16[512,5120]{1,0:T(8,128)(2,1)} %param.6, f32[512]{0:T(512)S(1)} %add_rsqrt_fusion.1, f32[512]{0:T(512)S(1)} %broadcast_multiply_fusion), kind=kOutput, calls=%fused_computation.29 | convolution fusion | flops 6722682368 | bytes 20977664 | tf_op jit(solution)/shard_map/dot_general | solution.py:44
  195.1 10.6 %psum.7 = f32[512]{0:T(512)S(1)} all-reduce(f32[512]{0:T(512)S(1)} %get-tuple-element.9), channel_id=1, replica_groups=mesh['bag'=64,'seq'=4] {'seq'}, use_global_device_ids=true, to_apply=%region_3.0 | all-reduce | flops 512 | bytes 4096 | tf_op jit(solution)/shard_map/psum | solution.py:45
  205.7 1.9 multiply_convert_fusion
  207.7 0.7 copy.29
  208.3 0.0 copy-start
  208.3 0.0 copy-start.1
  208.4 10.5 %fusion.31 = (f32[10,512]{1,0:T(8,128)S(1)}, f32[10,512,512]{1,2,0:T(8,128)}) fusion(pred[512]{0:T(512)(128)(4,1)S(1)} %iota_compare_fusion, bf16[512,10,128]{0,2,1:T(8,128)(2,1)S(1)} %bitcast.28, bf16[512,10,128]{0,2,1:T(8,128)(2,1)} %bitcast.31), kind=kOutput, calls=%fused_computation.44 | convolution fusion | flops 684196352 | bytes 13128192 | tf_op jit(solution)/shard_map/sub | solution.py:35
  218.9 0.0 copy-done
  218.9 0.0 copy-done.1
  218.9 6.4 %fusion.19 = f32[10,512,128]{1,2,0:T(8,128)} fusion(bf16[512,10,128]{0,2,1:T(8,128)(2,1)S(1)} %bitcast.30, f32[10,512,512]{1,2,0:T(8,128)} %get-tuple-element.14, f32[10,512]{1,0:T(8,128)S(1)} %get-tuple-element.13), kind=kOutput, calls=%fused_computation.26 | convolution fusion | flops 676331520 | bytes 14438400 | tf_op jit(solution)/shard_map/hts,shd->thd/dot_general | solution.py:37
  225.2 2.1 copy.40
  227.4 10.4 %fusion.30 = (f32[10,512]{1,0:T(8,128)S(1)}, f32[10,512,512]{1,2,0:T(8,128)}) fusion(pred[512]{0:T(512)(128)(4,1)S(1)} %iota_compare_fusion.1, bf16[512,10,128]{0,2,1:T(8,128)(2,1)} %bitcast.29, bf16[512,10,128]{0,2,1:T(8,128)(2,1)} %bitcast.33), kind=kOutput, calls=%fused_computation.43 | convolution fusion | flops 684196352 | bytes 13128192 | tf_op jit(solution)/shard_map/sub | solution.py:35
  237.8 6.8 %fusion.18 = f32[10,512,128]{1,2,0:T(8,128)} fusion(bf16[512,10,128]{0,2,1:T(8,128)(2,1)} %bitcast.32, f32[10,512,512]{1,2,0:T(8,128)} %get-tuple-element.12, f32[10,512]{1,0:T(8,128)S(1)} %get-tuple-element.11), kind=kOutput, calls=%fused_computation.25 | convolution fusion | flops 676331520 | bytes 14438400 | tf_op jit(solution)/shard_map/hts,shd->thd/dot_general | solution.py:37
  244.6 3.2 %copy.42 = f32[512,1280]{1,0:T(8,128)} copy(f32[512,1280]{0,1:T(8,128)} %bitcast.27) | data formatting | bytes 5242880 | tf_op jit(solution)/shard_map/reshape | solution.py:38
  247.8 3.1 %add_convert_fusion = bf16[512,1280]{1,0:T(8,128)(2,1)} fusion(f32[512,1280]{1,0:T(8,128)} %copy.42, f32[512,1280]{1,0:T(8,128)S(1)} %copy.40), kind=kLoop, calls=%fused_computation.27 | loop fusion | flops 2621440 | bytes 6553600 | tf_op jit(solution)/shard_map/convert_element_type | solution.py:50
  (5 shorter events, 0.0 us)
Async XLA Ops:
  6.5 83.0 %all-gather.5.cloned.1.call-start = ((), (), s32[]{:S(2)}) async-start(), calls=%async_computation.1 | async-start | bytes 2662400 | tf_op jit(solution)/shard_map/all_gather | solution.py:19
  7.3 173.9 %all-gather.3.cloned.1.call-start = ((), (), s32[]{:S(2)}) async-start(), calls=%async_computation | async-start | bytes 13312000 | tf_op jit(solution)/shard_map/all_gather | solution.py:43
  208.3 10.5 %copy-start = (bf16[512,1280]{0,1:T(8,128)(2,1)}, bf16[512,1280]{0,1:T(8,128)(2,1)S(1)}, u32[]{:S(2)}) copy-start(bf16[512,1280]{0,1:T(8,128)(2,1)S(1)} %copy.29) | copy-start | bytes 3932164
  208.3 10.5 %copy-start.1 = (bf16[1,512,1,1280]{1,3,2,0:T(8,128)(2,1)S(1)}, bf16[1,512,1,1280]{1,3,2,0:T(8,128)(2,1)}, u32[]{:S(2)}) copy-start(bf16[1,512,1,1280]{1,3,2,0:T(8,128)(2,1)} %copy.38) | copy-start | bytes 3932164
Sparse Core Ops, SparseCore 0:
  10.1 79.3 all-gather.4
  92.3 88.8 all-gather.2
where the time goes:
time: 259 us; the launch traced here: 258 us
  waiting for transfers between devices  131 us (51%)
  matrix products  48 us (19%)
  local copies, waits for them, and re-layouts  41.3 us (16%)
  between operations  14.7 us (6%)
  other arithmetic  12.4 us (5%)
  blocking collectives  10.6 us (4%)
    all_gather x1, waiting for transfers between devices, body(): gathered = lax.all_gather(w_query, 'bag', axis=0, tiled=True)  74 us
    all_gather x1, waiting for transfers between devices, negative_rows(): return lax.all_gather(neg_kv, 'bag', axis=0, tiled=True)  55.3 us
    sub x2, matrix products, attend(): weights = jnp.where(live, jnp.exp(scores - top), jnp.float32(0.0))  20.9 us
    dot_general x1, matrix products, body(): query = jnp.dot(normed, gathered, preferred_element_type=jnp.float32)  14 us
    dot_general x2, matrix products, attend(): jnp.einsum('hts,shd->thd', weights, v_heads, preferred_element_type=jnp.f...  13.1 us
    unnamed x6, local copies, waits for them, and re-layouts  12.4 us
    slice x2, local copies, waits for them, and re-layouts, body(): cond = attend(query_rms, cond_kv[0, :, 0], cond_kv[0, :, 1], prompt_len[0])  11.5 us
    slice x2, local copies, waits for them, and re-layouts, body(): uncond = attend(query_rms, negative[:, 0], negative[:, 1], neg_len[0])  11.4 us
  transfers between devices with their start and end apart: 2, of which 2 were waited for; matrix products, arithmetic and copies ran while one was open for 17% of the time, Pallas kernels for 0%

commit v1 on v0

--- a/solution.py
+++ b/solution.py
@@ -16,7 +16,9 @@
 
 
 def negative_rows(neg_kv):
-    return lax.all_gather(neg_kv, "bag", axis=0, tiled=True)
+    return jnp.concatenate(
+        lax.all_to_all(jnp.stack([neg_kv] * lax.axis_size("bag")), "bag", 0, 0), axis=0
+    )
 
 
 def attend(query_rms, keys, values, length):

time: 259 us -> 200 us (0.77)
  waiting for transfers between devices: 131 us -> 70.1 us
  local copies, waits for them, and re-layouts: 41.3 us -> 29.2 us
  starting transfers between devices: 0.04 us -> 12.1 us
    all_gather x1 -> x0, waiting for transfers between devices: 55.3 us -> none  [negative_rows(): return lax.all_gather(neg_kv, 'bag', axis=0, tiled=True)]
    all_gather x1, waiting for transfers between devices: 74 us -> 20.5 us  [body(): gathered = lax.all_gather(w_query, 'bag', axis=0, tiled=True)]
    all_to_all x0 -> x1, waiting for transfers between devices: none -> 48.9 us  [negative_rows(): lax.all_to_all(jnp.stack([neg_kv] * lax.axis_size('bag')), 'bag', 0, 0)]
    all_to_all x0 -> x1, starting transfers between devices: none -> 12.1 us  [negative_rows(): lax.all_to_all(jnp.stack([neg_kv] * lax.axis_size('bag')), 'bag', 0, 0)]
    slice x2 -> x3, local copies, waits for them, and re-layouts: 11.4 us -> 3.14 us  [body(): uncond = attend(query_rms, negative[:, 0], negative[:, 1], neg_len[0])]
    unnamed x6 -> x10, local copies, waits for them, and re-layouts: 12.4 us -> 7.11 us
  transfers between devices with their start and end apart: 2 -> 2, of which waited for: 2 -> 2; matrix products, arithmetic and copies ran while one was open for 17% -> 15% of each run, Pallas kernels for 0% -> 0%
where the time goes in v1:
time: 200 us; the launch traced here: 197 us
  waiting for transfers between devices  70.1 us (35%)
  matrix products  48 us (24%)
  local copies, waits for them, and re-layouts  29.2 us (15%)
  between operations  14.8 us (7%)
  other arithmetic  12.4 us (6%)
  starting transfers between devices  12.1 us (6%)
  blocking collectives  10.6 us (5%)
    all_to_all x1, waiting for transfers between devices, negative_rows(): lax.all_to_all(jnp.stack([neg_kv] * lax.axis_size('bag')), 'bag', 0, 0)  48.9 us
    sub x2, matrix products, attend(): weights = jnp.where(live, jnp.exp(scores - top), jnp.float32(0.0))  20.9 us
    all_gather x1, waiting for transfers between devices, body(): gathered = lax.all_gather(w_query, 'bag', axis=0, tiled=True)  20.5 us
    dot_general x1, matrix products, body(): query = jnp.dot(normed, gathered, preferred_element_type=jnp.float32)  14 us
    dot_general x2, matrix products, attend(): jnp.einsum('hts,shd->thd', weights, v_heads, preferred_element_type=jnp.f...  13.1 us
    all_to_all x1, starting transfers between devices, negative_rows(): lax.all_to_all(jnp.stack([neg_kv] * lax.axis_size('bag')), 'bag', 0, 0)  12.1 us
    psum x1, blocking collectives, body(): squares = lax.psum(jnp.sum(query * query, axis=1), 'seq')  10.6 us
    slice x2, local copies, waits for them, and re-layouts, body(): cond = attend(query_rms, cond_kv[0, :, 0], cond_kv[0, :, 1], prompt_len[0])  9.31 us
  transfers between devices with their start and end apart: 2, of which 2 were waited for; matrix products, arithmetic and copies ran while one was open for 15% of the time, Pallas kernels for 0%

profile of v1, /device:TPU:32, one launch (start us, length us, event | category | flops | bytes accessed | tf_op | source)
XLA Modules:
  0.0 197.2 jit_solution(7601800100922266700)
XLA Ops:
  6.5 0.0 all-gather.2.cloned.1.call-start
  6.5 0.7 all-gather.2.cloned.1.call-update
  7.3 0.8 copy.32
  8.0 1.6 stack.2
  9.7 0.0 copy-start
  9.7 12.1 %all-to-all-start = ((bf16[64,8,2,1280]{3,1,2,0:T(8,128)(2,1)}), bf16[64,8,2,1280]{3,1,2,0:T(8,128)(2,1)}, u32[]{:S(2)}, u32[]{:S(2)}) async-start(bf16[64,8,2,1280]{3,1,2,0:T(8,128)(2,1)} %stack.2), calls=%async_computation | async-start | bytes 5242880 | tf_op jit(solution)/shard_map/all_to_all | solution.py:20
  21.8 0.0 copy-done
  21.8 5.4 %fusion.28 = (bf16[1,512,1,1280]{3,2,1,0:T(2,128)(2,1)}, bf16[1,512,1,1280]{3,2,1,0:T(2,128)(2,1)}) fusion(bf16[1,512,2,1280]{3,2,1,0:T(2,128)(2,1)S(1)} %copy-done), kind=kLoop, calls=%fused_computation.42 | loop fusion | bytes 5242880 | tf_op jit(solution)/shard_map/slice | solution.py:50
  27.2 0.0 copy-start.1
  27.2 6.3 %copy.53 = bf16[1,512,1,1280]{1,3,2,0:T(8,128)(2,1)} copy(bf16[1,512,1,1280]{3,2,1,0:T(2,128)(2,1)} %get-tuple-element.5) | data formatting | bytes 2621440
  34.1 0.0 copy-done.1
  34.2 3.9 %copy.42 = bf16[1,512,1,1280]{1,3,2,0:T(8,128)(2,1)} copy(bf16[1,512,1,1280]{3,2,1,0:T(2,128)(2,1)S(1)} %copy-done.1) | data formatting | bytes 2621440 | tf_op jit(solution)/shard_map/slice | solution.py:50
  38.7 3.3 %convert_reduce_fusion = f32[512]{0:T(512)S(1)} fusion(bf16[512,5120]{1,0:T(8,128)(2,1)} %param.6), kind=kLoop, calls=%fused_computation.3 | loop fusion | flops 5242368 | bytes 5244928 | tf_op jit(solution)/shard_map/reduce_sum | solution.py:13
  42.0 4.0 %fusion.4 = f32[512]{0:T(512)S(1)} fusion(bf16[512,5120]{1,0:T(8,128)(2,1)} %param.6, f32[512]{0:T(512)S(1)} %broadcast_multiply_fusion), kind=kLoop, calls=%fused_computation.6 | loop fusion | flops 10485248 | bytes 5246976 | tf_op jit(solution)/shard_map/reduce_sum | solution.py:14
  46.0 48.9 %all-to-all-done = bf16[64,8,2,1280]{3,1,2,0:T(8,128)(2,1)} async-done(((bf16[64,8,2,1280]{3,1,2,0:T(8,128)(2,1)}), bf16[64,8,2,1280]{3,1,2,0:T(8,128)(2,1)}, u32[]{:S(2)}, u32[]{:S(2)}) %all-to-all-start) | async-done | bytes 2621472 | tf_op jit(solution)/shard_map/all_to_all | solution.py:20
  94.9 2.0 copy.55
  96.9 0.2 fusion.29
  97.1 1.5 copy.34
  98.6 1.5 copy.37
  100.0 20.5 %all-gather.2.cloned.1.call-done = bf16[5120,1280]{1,0:T(8,128)(2,1)} async-done(((bf16[80,1280]{1,0:T(8,128)(2,1)}), bf16[5120,1280]{1,0:T(8,128)(2,1)}) %all-gather.2.cloned.1.call-update) | async-done | bytes 13107216 | tf_op jit(solution)/shard_map/all_gather | solution.py:45
  120.5 14.0 %multiply_reduce_fusion = (f32[512]{0:T(512)S(1)}, f32[512,1280]{1,0:T(8,128)}) fusion(bf16[5120,1280]{1,0:T(8,128)(2,1)} %all-gather.2.cloned.1.call-done, bf16[512,5120]{1,0:T(8,128)(2,1)} %param.6, f32[512]{0:T(512)S(1)} %add_rsqrt_fusion.1, f32[512]{0:T(512)S(1)} %broadcast_multiply_fusion), kind=kOutput, calls=%fused_computation.30 | convolution fusion | flops 6722682368 | bytes 20977664 | tf_op jit(solution)/shard_map/dot_general | solution.py:46
  134.5 10.6 %psum.7 = f32[512]{0:T(512)S(1)} all-reduce(f32[512]{0:T(512)S(1)} %get-tuple-element.9), channel_id=1, replica_groups=mesh['bag'=64,'seq'=4] {'seq'}, use_global_device_ids=true, to_apply=%region_3.0 | all-reduce | flops 512 | bytes 4096 | tf_op jit(solution)/shard_map/psum | solution.py:47
  145.2 1.9 multiply_convert_fusion
  147.1 0.7 copy.31
  147.8 0.0 copy-start.2
  147.8 0.0 copy-start.3
  147.8 10.5 %fusion.31 = (f32[10,512]{1,0:T(8,128)S(1)}, f32[10,512,512]{1,2,0:T(8,128)}) fusion(pred[512]{0:T(512)(128)(4,1)S(1)} %iota_compare_fusion, bf16[512,10,128]{0,2,1:T(8,128)(2,1)S(1)} %bitcast.34, bf16[512,10,128]{0,2,1:T(8,128)(2,1)} %bitcast.36), kind=kOutput, calls=%fused_computation.45 | convolution fusion | flops 684196352 | bytes 13128192 | tf_op jit(solution)/shard_map/sub | solution.py:37
  158.3 0.0 copy-done.2
  158.3 0.0 copy-done.3
  158.3 6.4 %fusion.19 = f32[10,512,128]{1,2,0:T(8,128)} fusion(bf16[512,10,128]{0,2,1:T(8,128)(2,1)S(1)} %bitcast.37, f32[10,512,512]{1,2,0:T(8,128)} %get-tuple-element.14, f32[10,512]{1,0:T(8,128)S(1)} %get-tuple-element.13), kind=kOutput, calls=%fused_computation.26 | convolution fusion | flops 676331520 | bytes 14438400 | tf_op jit(solution)/shard_map/hts,shd->thd/dot_general | solution.py:39
  164.7 2.1 %copy.44 = f32[512,1280]{1,0:T(8,128)S(1)} copy(f32[512,1280]{0,1:T(8,128)} %bitcast.30) | data formatting | bytes 5242880 | tf_op jit(solution)/shard_map/reshape | solution.py:40
  166.8 10.4 %fusion.30 = (f32[10,512]{1,0:T(8,128)S(1)}, f32[10,512,512]{1,2,0:T(8,128)}) fusion(pred[512]{0:T(512)(128)(4,1)S(1)} %iota_compare_fusion.1, bf16[512,10,128]{0,2,1:T(8,128)(2,1)} %bitcast.35, bf16[512,10,128]{0,2,1:T(8,128)(2,1)} %bitcast.33), kind=kOutput, calls=%fused_computation.44 | convolution fusion | flops 684196352 | bytes 13128192 | tf_op jit(solution)/shard_map/sub | solution.py:37
  177.2 6.8 %fusion.18 = f32[10,512,128]{1,2,0:T(8,128)} fusion(bf16[512,10,128]{0,2,1:T(8,128)(2,1)} %bitcast.32, f32[10,512,512]{1,2,0:T(8,128)} %get-tuple-element.12, f32[10,512]{1,0:T(8,128)S(1)} %get-tuple-element.11), kind=kOutput, calls=%fused_computation.25 | convolution fusion | flops 676331520 | bytes 14438400 | tf_op jit(solution)/shard_map/hts,shd->thd/dot_general | solution.py:39
  184.0 3.2 %copy.46 = f32[512,1280]{1,0:T(8,128)} copy(f32[512,1280]{0,1:T(8,128)} %bitcast.31) | data formatting | bytes 5242880 | tf_op jit(solution)/shard_map/reshape | solution.py:40
  187.2 3.1 %add_convert_fusion = bf16[512,1280]{1,0:T(8,128)(2,1)} fusion(f32[512,1280]{1,0:T(8,128)} %copy.46, f32[512,1280]{1,0:T(8,128)S(1)} %copy.44), kind=kLoop, calls=%fused_computation.28 | loop fusion | flops 2621440 | bytes 6553600 | tf_op jit(solution)/shard_map/convert_element_type | solution.py:52
  (5 shorter events, 0.0 us)
Async XLA Ops:
  6.5 114.0 %all-gather.2.cloned.1.call-start = ((), (), s32[]{:S(2)}) async-start(), calls=%async_computation.1 | async-start | bytes 13312000 | tf_op jit(solution)/shard_map/all_gather | solution.py:45
  9.7 12.1 %copy-start = (bf16[1,512,2,1280]{3,2,1,0:T(2,128)(2,1)S(1)}, bf16[1,512,2,1280]{3,2,1,0:T(2,128)(2,1)}, u32[]{:S(2)}) copy-start(bf16[1,512,2,1280]{3,2,1,0:T(2,128)(2,1)} %param.8) | copy-start | bytes 7864324
  9.7 85.2 %all-to-all-start = ((bf16[64,8,2,1280]{3,1,2,0:T(8,128)(2,1)}), bf16[64,8,2,1280]{3,1,2,0:T(8,128)(2,1)}, u32[]{:S(2)}, u32[]{:S(2)}) async-start(bf16[64,8,2,1280]{3,1,2,0:T(8,128)(2,1)} %stack.2), calls=%async_computation | async-start | bytes 5242880 | tf_op jit(solution)/shard_map/all_to_all | solution.py:20
  27.2 7.0 %copy-start.1 = (bf16[1,512,1,1280]{3,2,1,0:T(2,128)(2,1)S(1)}, bf16[1,512,1,1280]{3,2,1,0:T(2,128)(2,1)}, u32[]{:S(2)}) copy-start(bf16[1,512,1,1280]{3,2,1,0:T(2,128)(2,1)} %get-tuple-element.6) | copy-start | bytes 3932164
  147.8 10.5 %copy-start.2 = (bf16[512,1280]{0,1:T(8,128)(2,1)}, bf16[512,1280]{0,1:T(8,128)(2,1)S(1)}, u32[]{:S(2)}) copy-start(bf16[512,1280]{0,1:T(8,128)(2,1)S(1)} %copy.31) | copy-start | bytes 3932164
  147.8 10.5 %copy-start.3 = (bf16[1,512,1,1280]{1,3,2,0:T(8,128)(2,1)S(1)}, bf16[1,512,1,1280]{1,3,2,0:T(8,128)(2,1)}, u32[]{:S(2)}) copy-start(bf16[1,512,1,1280]{1,3,2,0:T(8,128)(2,1)} %copy.42) | copy-start | bytes 3932164
Sparse Core Ops, SparseCore 0:
  10.1 110.4 all-gather.1
